TPU v7x, 32 devices: a whole 2x2x4 slice. The times are simulated.
32 devices in a mesh: fsdp: 8 (over z, x), head: 2 (over core), tensor: 2 (over y).
Axes of the slice: x: 2, y: 2, z: 4, core: 2. Of those that a mesh axis runs over, the one named last changes fastest.
Arguments:
- block_in: bfloat16 [4096, 1024], P('fsdp'), may hold values from -6 to 6
- cotangent: bfloat16 [4096, 1024], P('fsdp'), may hold values from -6 to 6
- norm_gain: float32 [1024], replicated, may hold values from 0.5 to 1.5
- w_x: bfloat16 [1024, 32, 64], P('fsdp', 'head', 'tensor'), may hold values from -0.1875 to 0.1875
- w_z: bfloat16 [1024, 32, 64], P('fsdp', 'head', 'tensor'), may hold values from -0.1875 to 0.1875
- w_bc: bfloat16 [1024, 2, 128], P('fsdp'), may hold values from -0.1875 to 0.1875
- w_dt: bfloat16 [1024, 32], P('fsdp', 'head'), may hold values from -0.1875 to 0.1875
- conv_x: float32 [32, 64, 4], P('head', 'tensor'), may hold values from -3 to 3
- conv_bc: float32 [2, 128, 4], replicated, may hold values from -3 to 3
- dt_bias: float32 [32], P('head'), may hold values from -6 to -2
- a_log: float32 [32], P('head'), may hold values from -1.5 to 0.5
- skip: float32 [32], P('head'), may hold values from 0.5 to 1.5
- gate_gain: float32 [32, 64], P('head', 'tensor'), may hold values from 0.5 to 1.5
- w_out: bfloat16 [32, 64, 1024], P('head', 'tensor', 'fsdp'), may hold values from -0.125 to 0.125
Outputs:
- block_out: bfloat16 [4096, 1024], P('fsdp')
- grad_in: float32 [4096, 1024], P('fsdp')
- grad_norm_gain: float32 [1024], replicated
- grad_w_x: float32 [1024, 32, 64], P('fsdp', 'head', 'tensor')
- grad_w_z: float32 [1024, 32, 64], P('fsdp', 'head', 'tensor')
- grad_w_bc: float32 [1024, 2, 128], P('fsdp')
- grad_w_dt: float32 [1024, 32], P('fsdp', 'head')
- grad_conv_x: float32 [32, 64, 4], P('head', 'tensor')
- grad_conv_bc: float32 [2, 128, 4], replicated
- grad_dt_bias: float32 [32], P('head')
- grad_a_log: float32 [32], P('head')
- grad_skip: float32 [32], P('head')
- grad_gate_gain: float32 [32, 64], P('head', 'tensor')
- grad_w_out: float32 [32, 64, 1024], P('head', 'tensor', 'fsdp')
All inputs are finite; a program needn't handle non-finite values.
Results may differ from a plain program's by a relative error of at most 0.011.
Values may be sent and summed in bfloat16 or wider, within the bound.
A program may use at most 128 MiB of HBM per device.

v0:
```python
from functools import partial
import jax
import jax.numpy as jnp
from jax import lax
from jax.sharding import PartitionSpec as P

SPAN = 256
EPSILON = 1e-05
PRECISE = lax.Precision.HIGHEST


def causal_conv(signal, kernel):
    taps = kernel.shape[1]
    length = signal.shape[0]
    padded = jnp.pad(signal, ((taps - 1, 0), (0, 0)))
    total = jnp.zeros_like(signal)
    for offset in range(taps):
        total = total + padded[offset : offset + length] * kernel[:, offset]
    return total


def conv_silu(signal, kernel):
    return jax.nn.silu(causal_conv(signal, kernel))


def silu_slope(value):
    sigma = jax.nn.sigmoid(value)
    return sigma * (1.0 + value * (1.0 - sigma))


def scan_spans(values, step_size, rate, b_maps, c_maps, block):
    length, head_count, channels = values.shape
    blocks = length // block
    logs = (step_size * rate).reshape(blocks, block, head_count)
    cums = jnp.cumsum(logs, axis=1)
    x_blocks = values.reshape(blocks, block, head_count, channels)
    dt_blocks = step_size.reshape(blocks, block, head_count)
    b_blocks = b_maps.reshape(blocks, block, -1)
    c_blocks = c_maps.reshape(blocks, block, -1)
    scores = jnp.einsum("cln,csn->cls", c_blocks, b_blocks, precision=PRECISE)
    causal = (jnp.arange(block)[:, None] >= jnp.arange(block)[None, :])[None, :, :, None]
    gaps = cums[:, :, None, :] - cums[:, None, :, :]
    decays = jnp.where(causal, jnp.exp(jnp.where(causal, gaps, 0.0)), 0.0)
    mixing = scores[..., None] * decays * dt_blocks[:, None, :, :]
    intra_part = jnp.einsum("clsh,cshp->clhp", mixing, x_blocks, precision=PRECISE)
    to_end = jnp.exp(cums[:, -1:, :] - cums) * dt_blocks
    states = jnp.einsum("csh,csn,cshp->chpn", to_end, b_blocks, x_blocks, precision=PRECISE)
    whole_decay = jnp.exp(cums[:, -1, :])
    carried = []
    running = jnp.zeros_like(states[0])
    for position in range(blocks):
        carried.append(running)
        running = running * whole_decay[position][:, None, None] + states[position]
    entering = jnp.stack(carried)
    inter_part = jnp.einsum(
        "cln,clh,chpn->clhp", c_blocks, jnp.exp(cums), entering, precision=PRECISE
    )
    return (intra_part + inter_part).reshape(length, head_count, channels)


def mixer(values, dt_raw, dt_bias, a_log, skip, b_maps, c_maps, block):
    step_size = jax.nn.softplus(dt_raw + dt_bias)
    rate = -jnp.exp(a_log)
    return scan_spans(values, step_size, rate, b_maps, c_maps, block) + skip[:, None] * values


def on_device(
    block_in,
    cotangent,
    norm_gain,
    w_x,
    w_z,
    w_bc,
    w_dt,
    conv_x,
    conv_bc,
    dt_bias,
    a_log,
    skip,
    gate_gain,
    w_out,
):
    length, model_width = block_in.shape
    head_count, head_width, taps = conv_x.shape
    state_size = conv_bc.shape[1]
    inner_width = head_count * head_width
    group_count = lax.axis_size("head") * lax.axis_size("tensor")
    full_inner = inner_width * group_count
    weights = (w_x, w_z, w_bc, w_dt, w_out)
    gathered = (
        lax.all_gather(weights[0], "fsdp", axis=0, tiled=True),
        lax.all_gather(weights[1], "fsdp", axis=0, tiled=True),
        lax.all_gather(weights[2], "fsdp", axis=0, tiled=True),
        lax.all_gather(weights[3], "fsdp", axis=0, tiled=True),
        lax.all_gather(weights[4], "fsdp", axis=2, tiled=True),
    )
    weight_x = gathered[0].reshape(model_width, inner_width)
    weight_z = gathered[1].reshape(model_width, inner_width)
    weight_bc = gathered[2].reshape(model_width, 2 * state_size)
    weight_dt = gathered[3]
    weight_out = gathered[4].reshape(inner_width, model_width)
    kernel_x = conv_x.reshape(inner_width, taps)
    kernel_bc = conv_bc.reshape(2 * state_size, taps)
    gain_flat = gate_gain.reshape(inner_width)
    features = block_in.astype(jnp.float32)
    scale_in = lax.rsqrt(jnp.mean(features * features, axis=1, keepdims=True) + EPSILON)
    normed = (features * scale_in * norm_gain).astype(jnp.bfloat16)
    x_raw = jnp.dot(normed, weight_x, preferred_element_type=jnp.float32)
    z_raw = jnp.dot(normed, weight_z, preferred_element_type=jnp.float32)
    bc_raw = jnp.dot(normed, weight_bc, preferred_element_type=jnp.float32)
    dt_raw = jnp.dot(normed, weight_dt, preferred_element_type=jnp.float32)
    x_act = conv_silu(x_raw, kernel_x).astype(jnp.bfloat16)
    bc_act = conv_silu(bc_raw, kernel_bc).astype(jnp.bfloat16)
    values = x_act.astype(jnp.float32).reshape(length, head_count, head_width)
    b_maps = bc_act[:, :state_size].astype(jnp.float32)
    c_maps = bc_act[:, state_size:].astype(jnp.float32)
    mixed = mixer(values, dt_raw, dt_bias, a_log, skip, b_maps, c_maps, SPAN).reshape(
        length, inner_width
    )
    gated = mixed * jax.nn.silu(z_raw)
    square_sum = lax.psum(jnp.sum(gated * gated, axis=1), ("head", "tensor"))
    scale_out = lax.rsqrt(square_sum / full_inner + EPSILON)[:, None]
    normed_out = (gated * scale_out * gain_flat).astype(jnp.bfloat16)
    partial_out = jnp.dot(normed_out, weight_out, preferred_element_type=jnp.float32)
    summed = lax.psum(partial_out, ("head", "tensor"))
    block_out = (summed + features).astype(jnp.bfloat16)
    again = (
        lax.all_gather(weights[0], "fsdp", axis=0, tiled=True),
        lax.all_gather(weights[1], "fsdp", axis=0, tiled=True),
        lax.all_gather(weights[2], "fsdp", axis=0, tiled=True),
        lax.all_gather(weights[3], "fsdp", axis=0, tiled=True),
        lax.all_gather(weights[4], "fsdp", axis=2, tiled=True),
    )
    back_x = again[0].reshape(model_width, inner_width)
    back_z = again[1].reshape(model_width, inner_width)
    back_bc = again[2].reshape(model_width, 2 * state_size)
    back_dt = again[3]
    back_out = again[4].reshape(inner_width, model_width)
    upstream = cotangent.astype(jnp.float32)
    d_normed_out = jnp.dot(cotangent, back_out.T, preferred_element_type=jnp.float32)
    g_w_out = jnp.dot(normed_out.T, cotangent, preferred_element_type=jnp.float32)
    g_gate_gain = jnp.sum(d_normed_out * gated * scale_out, axis=0)
    d_hat = d_normed_out * gain_flat
    inner_sum = lax.psum(jnp.sum(d_hat * gated, axis=1), ("head", "tensor"))[:, None]
    d_gated = scale_out * d_hat - gated * scale_out**3 * inner_sum / full_inner
    d_mixed = d_gated * jax.nn.silu(z_raw)
    d_z = (d_gated * mixed * silu_slope(z_raw)).astype(jnp.bfloat16)
    _, pullback = jax.vjp(
        partial(mixer, block=SPAN), values, dt_raw, dt_bias, a_log, skip, b_maps, c_maps
    )
    d_xs, d_dt, g_dt_bias, g_a_log, g_skip, d_b, d_c = pullback(
        d_mixed.reshape(length, head_count, head_width)
    )
    d_dt, g_dt_bias, g_a_log, g_skip = lax.psum((d_dt, g_dt_bias, g_a_log, g_skip), "tensor")
    d_bc = lax.psum(jnp.concatenate([d_b, d_c], axis=1), ("head", "tensor"))
    _, pull_x = jax.vjp(conv_silu, x_raw, kernel_x)
    d_x_raw, g_conv_x = pull_x(d_xs.reshape(length, inner_width))
    _, pull_bc = jax.vjp(conv_silu, bc_raw, kernel_bc)
    d_bc_raw, g_conv_bc = pull_bc(d_bc)
    d_x_b = d_x_raw.astype(jnp.bfloat16)
    d_bc_b = d_bc_raw.astype(jnp.bfloat16)
    d_dt_b = d_dt.astype(jnp.bfloat16)
    g_w_x = jnp.dot(normed.T, d_x_b, preferred_element_type=jnp.float32)
    g_w_z = jnp.dot(normed.T, d_z, preferred_element_type=jnp.float32)
    g_w_bc = jnp.dot(normed.T, d_bc_b, preferred_element_type=jnp.float32)
    g_w_dt = jnp.dot(normed.T, d_dt_b, preferred_element_type=jnp.float32)
    local_part = (
        jnp.dot(d_x_b, back_x.T, preferred_element_type=jnp.float32)
        + jnp.dot(d_z, back_z.T, preferred_element_type=jnp.float32)
        + jnp.dot(d_dt_b, back_dt.T, preferred_element_type=jnp.float32)
        * (1.0 / lax.axis_size("tensor"))
    )
    d_normed = lax.psum(local_part, ("head", "tensor")) + jnp.dot(
        d_bc_b, back_bc.T, preferred_element_type=jnp.float32
    )
    g_norm_gain = jnp.sum(d_normed * features * scale_in, axis=0)
    d_in_hat = d_normed * norm_gain
    grad_in = (
        scale_in * d_in_hat
        - features * scale_in**3 * jnp.mean(d_in_hat * features, axis=1, keepdims=True)
        + upstream
    )
    big_grads = (
        lax.psum_scatter(
            g_w_x.reshape(model_width, head_count, head_width),
            "fsdp",
            scatter_dimension=0,
            tiled=True,
        ),
        lax.psum_scatter(
            g_w_z.reshape(model_width, head_count, head_width),
            "fsdp",
            scatter_dimension=0,
            tiled=True,
        ),
        lax.psum_scatter(g_w_bc, "fsdp", scatter_dimension=0, tiled=True),
        lax.psum_scatter(g_w_dt, "fsdp", scatter_dimension=0, tiled=True),
        lax.psum_scatter(
            g_w_out.reshape(head_count, head_width, model_width),
            "fsdp",
            scatter_dimension=2,
            tiled=True,
        ),
    )
    owned_bc = big_grads[2].reshape(-1, 2, state_size)
    small = lax.psum(
        (
            g_norm_gain,
            g_conv_x.reshape(head_count, head_width, taps),
            g_conv_bc.reshape(2, state_size, taps),
            g_dt_bias,
            g_a_log,
            g_skip,
            g_gate_gain.reshape(head_count, head_width),
        ),
        "fsdp",
    )
    return (
        block_out,
        grad_in,
        small[0],
        big_grads[0],
        big_grads[1],
        owned_bc,
        big_grads[3],
        small[1],
        small[2],
        small[3],
        small[4],
        small[5],
        small[6],
        big_grads[4],
    )


def solution(mesh):
    return jax.shard_map(
        on_device,
        mesh=mesh,
        in_specs=(
            P("fsdp", None),
            P("fsdp", None),
            P(),
            P("fsdp", "head", "tensor"),
            P("fsdp", "head", "tensor"),
            P("fsdp", None, None),
            P("fsdp", "head"),
            P("head", "tensor", None),
            P(),
            P("head"),
            P("head"),
            P("head"),
            P("head", "tensor"),
            P("head", "tensor", "fsdp"),
        ),
        out_specs=(
            P("fsdp", None),
            P("fsdp", None),
            P(),
            P("fsdp", "head", "tensor"),
            P("fsdp", "head", "tensor"),
            P("fsdp", None, None),
            P("fsdp", "head"),
            P("head", "tensor", None),
            P(),
            P("head"),
            P("head"),
            P("head"),
            P("head", "tensor"),
            P("head", "tensor", "fsdp"),
        ),
        check_vma=False,
    )
```

profile of v0, /device:TPU:0, one launch (start us, length us, event | category | flops | bytes accessed | tf_op | source)
XLA Modules:
  0.0 668.9 jit_solution(9409954152697508148)
XLA Ops:
  8.0 0.7 all-gather.6.cloned.1.call-update
  10.8 1.6 fusion.22
  13.0 28.3 %all_gather.22 = bf16[1024,16]{0,1:T(8,128)(2,1)S(1)} all-gather(bf16[128,16]{0,1:T(8,128)(2,1)} %param.20), channel_id=1, replica_groups=mesh['fsdp'=8,'head'=2,'tensor'=2] {'fsdp'}, dimensions={0}, use_global_device_ids=true | all-gather | bytes 36864 | tf_op jit(solution)/shard_map/all_gather | solution.py:94
  41.3 2.3 broadcast_multiply_fusion.8
  43.6 1.2 reduce-window.14
  45.9 0.7 fusion.91
  48.1 32.0 %all_gather.21 = bf16[1024,2,128]{2,1,0:T(2,128)(2,1)S(1)} all-gather(bf16[128,2,128]{2,1,0:T(2,128)(2,1)S(1)} %copy-done.27), channel_id=1, replica_groups=mesh['fsdp'=8,'head'=2,'tensor'=2] {'fsdp'}, dimensions={0}, use_global_device_ids=true | all-gather | bytes 589824 | tf_op jit(solution)/shard_map/all_gather | solution.py:93
  80.1 0.8 copy-done.9
  81.4 1.1 multiply_convert_fusion.3
  82.9 2.2 fusion.105
  85.1 0.9 copy-done.4
  86.0 1.6 multiply_convert_fusion.2
  88.0 1.3 convolution_add_fusion.3
  90.0 6.3 fusion.38
  96.3 0.8 copy.135
  97.2 1.3 copy.136
  98.5 3.5 multiply_reduce_fusion.9
  102.1 7.9 %psum.112 = f32[512]{0:T(512)S(1)} all-reduce(f32[512]{0:T(512)S(1)} %get-tuple-element.106), channel_id=1, replica_groups=mesh['fsdp'=8,'head'=2,'tensor'=2] {'head','tensor'}, use_global_device_ids=true, to_apply=%region_4.5 | all-reduce | flops 512 | bytes 4096 | tf_op jit(solution)/shard_map/psum | solution.py:121
  110.0 25.5 %all-gather.8.cloned.1.call-done = bf16[16,32,1024]{2,1,0:T(8,128)(2,1)} async-done(((bf16[16,32,128]{2,1,0:T(8,128)(2,1)}), bf16[16,32,1024]{2,1,0:T(8,128)(2,1)}) %all-gather.8.cloned.1.call-update) | async-done | bytes 1048592 | tf_op jit(solution)/shard_map/all_gather | solution.py:95
  135.5 3.9 multiply_reduce_fusion.3
  139.4 7.5 %psum.114 = f32[512]{0:T(512)S(1)} all-reduce(f32[512]{0:T(512)S(1)} %get-tuple-element.77), channel_id=1, replica_groups=mesh['fsdp'=8,'head'=2,'tensor'=2] {'head','tensor'}, use_global_device_ids=true, to_apply=%region_7.8 | all-reduce | flops 512 | bytes 4096 | tf_op jit(solution)/shard_map/psum | solution.py:144
  146.9 4.2 fusion.45
  151.2 1.3 copy.137
  152.5 2.9 reshape_reshape.8
  155.4 1.9 multiply_reduce_fusion.1
  157.3 2.6 convolution_bitcast_fusion.1
  159.8 1.0 multiply_reduce_fusion.14
  160.8 2.6 convolution_bitcast_fusion.2
  164.0 11.4 %fusion.9 = (f32[2,256,16]{1,2,0:T(8,128)}, f32[2,256,16]{1,2,0:T(8,128)}, f32[2,256,16]{1,2,0:T(8,128)}, f32[2,256,256]{2,1,0:T(8,128)}) fusion(f32[2,256,16]{1,2,0:T(8,128)S(1)} %bitcast.241, f32[2,256,16]{1,2,0:T(8,128)S(1)} %copy-done.26, f32[2,256,256]{2,1,0:T(8,128)S(1)} %copy-done.20, pred[256,256]{1,0:T(8,128)(4,1)S(1)} %copy-done.29, ...), kind=kOutput, calls=%fused_computation.18 | convolution fusion | flops 836608000 | bytes 2850816 | tf_op jit(solution)/shard_map/transpose(jvp(clsh,cshp->clhp))/dot_general | solution.py:45
  175.5 8.0 %fusion.41 = f32[2,256,16,32]{1,3,2,0:T(8,128)} fusion(f32[2,256,16]{1,2,0:T(8,128)S(1)} %bitcast.242, f32[2,256,16]{1,2,0:T(8,128)S(1)} %copy-done.26, f32[2,256,256]{2,1,0:T(8,128)S(1)} %copy-done.20, pred[256,256]{1,0:T(8,128)(4,1)S(1)} %copy-done.29, f32[2,256,16,32]{1,3,2,0:T(8,128)S(1)} %fusion.58, f32[2,16,32,256]{3,0,2,1:T(2,128)S(1)} %bitcast.207, ...), kind=kOutput, calls=%fused_computation.48 | convolution fusion | flops 816316416 | bytes 3833856 | tf_op jit(solution)/shard_map/transpose(jvp(clsh,cshp->clhp))/dot_general | solution.py:45
  183.5 0.9 multiply_reduce_fusion.2
  184.7 2.1 fusion.93
  186.8 0.8 reduce_sum.252
  188.2 1.2 multiply_bitcast_fusion
  189.4 0.8 copy.145
  190.2 2.5 convolution_add_fusion.2
  192.7 2.2 convolution_add_fusion.1
  194.9 0.8 copy.140
  195.8 1.0 copy.178
  196.9 2.6 copy.141
  199.9 5.0 reduce-window.16
  205.3 3.6 fusion.118
  209.0 0.9 multiply_reduce_fusion.7
  211.7 2.0 fusion.117
  213.8 0.8 pad_maximum_fusion
  214.6 8.2 %all-reduce.25 = (bf16[512,16]{0,1:T(8,128)(2,1)S(1)}, f32[16]{0:T(128)S(1)}, f32[16]{0:T(128)S(1)}, f32[16]{0:T(128)S(1)}) all-reduce(f32[512,16]{0,1:T(8,128)S(1)} %get-tuple-element.105, f32[16]{0:T(128)S(1)} %get-tuple-element.104, f32[16]{0:T(128)S(1)} %negate_multiply_fusion, ...), channel_id=1, replica_groups=mesh['fsdp'=8,'head'=2,'tensor'=2] {'tensor'}, use_global_device_ids=true, to_apply=%region_15.16 | all-reduce | flops 8240 | bytes 49536 | tf_op jit(solution)/shard_map/psum | solution.py:154
  222.8 4.0 multiply_add_fusion
  227.0 92.6 %all-reduce.28.cloned.1.call-done = (f32[512,1024]{1,0:T(8,128)}, f32[512,1024]{1,0:T(8,128)}, f32[512,256]{1,0:T(8,128)}) async-done(((f32[512,1024]{1,0:T(8,128)}, f32[512,1024]{1,0:T(8,128)}, f32[512,256]{1,0:T(8,128)}), (f32[512,1024]{1,0:T(8,128)}, f32[512,1024]{1,0:T(8,128)}, f32[512,256]{1,0:T(8,128)})) %all-reduce.28.cloned.1.call-update) | async-done | bytes 4718608 | tf_op jit(solution)/shard_map/psum | solution.py:125
  319.5 1.6 multiply_reduce_fusion.13
  321.9 1.6 fusion.95
  323.5 1.1 fusion.82
  324.7 3.4 fusion.92
  328.1 1.0 copy-done.3
  329.1 2.2 fusion.97
  331.4 2.2 fusion.99
  333.8 2.6 fusion.31
  336.5 38.1 %all-reduce.23 = (f32[1024]{0:T(1024)}, f32[16,32,4]{1,0,2:T(8,128)S(1)}, f32[2,128,4]{1,2,0:T(4,128)}, f32[16]{0:T(128)}, f32[16]{0:T(128)}, /*index=5*/f32[16]{0:T(128)}, f32[16,32]{1,0:T(8,128)}) all-reduce(f32[1024]{0:T(1024)S(1)} %get-tuple-element.74, ...), channel_id=1, replica_groups=mesh['fsdp'=8,'head'=2,'tensor'=2] {'fsdp'}, use_global_device_ids=true, to_apply=%region_21.22 | all-reduce | flops 4656 | bytes 37248 | tf_op jit(solution)/shard_map/psum | solution.py:206
  375.3 4.3 fusion.28
  379.6 8.5 %reduce-scatter.10.cloned.1.call-done = f32[128,256]{1,0:T(8,128)} async-done(((f32[1024,256]{1,0:T(8,128)}), f32[128,256]{1,0:T(8,128)}) %reduce-scatter.10.cloned.1.call-update) | async-done | bytes 131088 | tf_op jit(solution)/shard_map/reduce_scatter | solution.py:196
  388.1 1.6 reshape.276
  389.7 55.8 %reduce-scatter.12.cloned.1.call-done = f32[128,16]{0,1:T(8,128)} async-done(((f32[1024,16]{0,1:T(8,128)}), f32[128,16]{0,1:T(8,128)}) %reduce-scatter.12.cloned.1.call-update) | async-done | bytes 8208 | tf_op jit(solution)/shard_map/reduce_scatter | solution.py:197
  445.5 72.4 %reduce-scatter.14.cloned.1.call-done = f32[16,32,128]{2,1,0:T(8,128)} async-done(((f32[16,32,1024]{2,1,0:T(8,128)}), f32[16,32,128]{2,1,0:T(8,128)}) %reduce-scatter.14.cloned.1.call-update) | async-done | bytes 262160 | tf_op jit(solution)/shard_map/reduce_scatter | solution.py:198
  517.9 72.0 %reduce-scatter.8.cloned.1.call-done = f32[128,16,32]{0,2,1:T(8,128)} async-done(((f32[1024,16,32]{0,2,1:T(8,128)}), f32[128,16,32]{0,2,1:T(8,128)}) %reduce-scatter.8.cloned.1.call-update) | async-done | bytes 262160 | tf_op jit(solution)/shard_map/reduce_scatter | solution.py:190
  590.0 72.1 %reduce-scatter.6.cloned.1.call-done = f32[128,16,32]{0,2,1:T(8,128)} async-done(((f32[1024,16,32]{0,2,1:T(8,128)}), f32[128,16,32]{0,2,1:T(8,128)}) %reduce-scatter.6.cloned.1.call-update) | async-done | bytes 262160 | tf_op jit(solution)/shard_map/reduce_scatter | solution.py:184
  (221 shorter events, 13.8 us)
Async XLA Ops:
  7.2 39.4 %copy-start.69 = (f32[16,32]{1,0:T(8,128)S(1)}, f32[16,32]{1,0:T(8,128)}, u32[]{:S(2)}) copy-start(f32[16,32]{1,0:T(8,128)} %param.26) | copy-start | bytes 6148
  7.2 39.5 %copy-start.70 = (f32[2,128,4]{1,2,0:T(4,128)S(1)}, f32[2,128,4]{1,2,0:T(4,128)}, u32[]{:S(2)}) copy-start(f32[2,128,4]{1,2,0:T(4,128)} %param.22) | copy-start | bytes 12292
  7.2 39.5 %copy-start.75 = (f32[16]{0:T(128)S(1)}, f32[16]{0:T(128)}, u32[]{:S(2)}) copy-start(f32[16]{0:T(128)} %param.25) | copy-start | bytes 196
  7.2 40.2 %copy-start.45 = (f32[16,32,4]{1,2,0:T(4,128)S(1)}, f32[16,32,4]{1,2,0:T(4,128)}, u32[]{:S(2)}) copy-start(f32[16,32,4]{1,2,0:T(4,128)} %param.21) | copy-start | bytes 24580
  7.2 40.9 %copy-start.27 = (bf16[128,2,128]{2,1,0:T(2,128)(2,1)S(1)}, bf16[128,2,128]{2,1,0:T(2,128)(2,1)}, u32[]{:S(2)}) copy-start(bf16[128,2,128]{2,1,0:T(2,128)(2,1)} %param.19) | copy-start | bytes 196612
  7.2 75.6 %all-gather.4.cloned.1.call-start = ((), (), s32[]{:S(2)}) async-start(), calls=%async_computation.5 | async-start | bytes 1179648 | tf_op jit(solution)/shard_map/all_gather | solution.py:91
  8.0 90.6 %all-gather.6.cloned.1.call-start = ((), (), s32[]{:S(2)}) async-start(), calls=%async_computation.6 | async-start | bytes 1179648 | tf_op jit(solution)/shard_map/all_gather | solution.py:92
  8.7 126.8 %all-gather.8.cloned.1.call-start = ((), (), s32[]{:S(2)}) async-start(), calls=%async_computation.7 | async-start | bytes 1179648 | tf_op jit(solution)/shard_map/all_gather | solution.py:95
  9.4 310.1 %all-reduce.28.cloned.1.call-start = ((), (), s32[]{:S(2)}) async-start(), calls=%async_computation.13 | async-start | bytes 9437184 | tf_op jit(solution)/shard_map/psum | solution.py:125
  10.8 35.8 %copy-start.73 = (f32[16]{0:T(128)}, f32[16]{0:T(128)S(1)}, u32[]{:S(2)}) copy-start(f32[16]{0:T(128)S(1)} %exponential_negate_fusion) | copy-start | bytes 196
  10.8 70.1 %copy-start = (bf16[512,1024]{1,0:T(8,128)(2,1)S(1)}, bf16[512,1024]{1,0:T(8,128)(2,1)}, u32[]{:S(2)}) copy-start(bf16[512,1024]{1,0:T(8,128)(2,1)} %param.14) | copy-start | bytes 3145732
  10.8 70.1 %copy-start.30 = (f32[1024]{0:T(1024)S(1)}, f32[1024]{0:T(1024)}, u32[]{:S(2)}) copy-start(f32[1024]{0:T(1024)} %param.16) | copy-start | bytes 12292
  13.0 85.6 %copy-start.32 = (f32[512]{0:T(512)}, f32[512]{0:T(512)S(1)}, u32[]{:S(2)}) copy-start(f32[512]{0:T(512)S(1)} %get-tuple-element.141) | copy-start | bytes 6148
  41.3 2.3 copy-start.23
  45.0 37.6 %copy-start.34 = (f32[2,16,2]{1,2,0:T(2,128)}, f32[2,16,2]{1,2,0:T(2,128)S(1)}, u32[]{:S(2)}) copy-start(f32[2,16,2]{1,2,0:T(2,128)S(1)} %slice.130) | copy-start | bytes 772
  45.0 44.9 %copy-start.25 = (f32[2,256,16]{1,2,0:T(8,128)}, f32[2,256,16]{1,2,0:T(8,128)S(1)}, u32[]{:S(2)}) copy-start(f32[2,256,16]{1,2,0:T(8,128)S(1)} %bitcast_bitcast_fusion.1) | copy-start | bytes 98308
  45.2 143.0 %copy-start.36 = (f32[2,16]{1,0:T(2,128)}, f32[2,16]{1,0:T(2,128)S(1)}, u32[]{:S(2)}) copy-start(f32[2,16]{1,0:T(2,128)S(1)} %slice_reduce_fusion.2) | copy-start | bytes 388
  46.6 137.8 %copy-start.38 = (f32[512]{0:T(512)}, f32[512]{0:T(512)S(1)}, u32[]{:S(2)}) copy-start(f32[512]{0:T(512)S(1)} %mul.547) | copy-start | bytes 6148
  46.7 35.9 %copy-start.60 = (f32[256,1]{0,1:T(1,128)}, f32[256,1]{0,1:T(1,128)S(1)}, u32[]{:S(2)}) copy-start(f32[256,1]{0,1:T(1,128)S(1)} %get-tuple-element.136) | copy-start | bytes 3076
  46.7 35.9 %copy-start.62 = (f32[256,1]{0,1:T(1,128)}, f32[256,1]{0,1:T(1,128)S(1)}, u32[]{:S(2)}) copy-start(f32[256,1]{0,1:T(1,128)S(1)} %get-tuple-element.137) | copy-start | bytes 3076
  46.7 35.9 %copy-start.64 = (f32[256,1]{0,1:T(1,128)}, f32[256,1]{0,1:T(1,128)S(1)}, u32[]{:S(2)}) copy-start(f32[256,1]{0,1:T(1,128)S(1)} %get-tuple-element.138) | copy-start | bytes 3076
  46.7 35.8 %copy-start.66 = (f32[256,1]{0,1:T(1,128)}, f32[256,1]{0,1:T(1,128)S(1)}, u32[]{:S(2)}) copy-start(f32[256,1]{0,1:T(1,128)S(1)} %get-tuple-element.139) | copy-start | bytes 3076
  47.5 37.5 %copy-start.50 = (f32[512,1]{0,1:T(1,128)}, f32[512,1]{0,1:T(1,128)S(1)}, u32[]{:S(2)}) copy-start(f32[512,1]{0,1:T(1,128)S(1)} %get-tuple-element.132) | copy-start | bytes 6148
  47.6 37.5 %copy-start.52 = (f32[512,1]{0,1:T(1,128)}, f32[512,1]{0,1:T(1,128)S(1)}, u32[]{:S(2)}) copy-start(f32[512,1]{0,1:T(1,128)S(1)} %get-tuple-element.133) | copy-start | bytes 6148
  47.6 37.5 %copy-start.54 = (f32[512,1]{0,1:T(1,128)}, f32[512,1]{0,1:T(1,128)S(1)}, u32[]{:S(2)}) copy-start(f32[512,1]{0,1:T(1,128)S(1)} %get-tuple-element.134) | copy-start | bytes 6148
  47.6 37.5 %copy-start.56 = (f32[512,1]{0,1:T(1,128)}, f32[512,1]{0,1:T(1,128)S(1)}, u32[]{:S(2)}) copy-start(f32[512,1]{0,1:T(1,128)S(1)} %get-tuple-element.135) | copy-start | bytes 6148
  82.8 7.1 %copy-start.19 = (f32[2,256,256]{2,1,0:T(8,128)}, f32[2,256,256]{2,1,0:T(8,128)S(1)}, u32[]{:S(2)}) copy-start(f32[2,256,256]{2,1,0:T(8,128)S(1)} %fusion.116) | copy-start | bytes 1572868
  87.6 11.0 %copy-start.2 = (bf16[512,512]{1,0:T(8,128)(2,1)}, bf16[512,512]{1,0:T(8,128)(2,1)S(1)}, u32[]{:S(2)}) copy-start(bf16[512,512]{1,0:T(8,128)(2,1)S(1)} %get-tuple-element.108) | copy-start | bytes 1572868
  87.9 8.4 %copy-start.10 = (bf16[2,256,16,32]{1,0,3,2:T(2,128)(2,1)}, bf16[2,256,16,32]{1,0,3,2:T(2,128)(2,1)S(1)}, u32[]{:S(2)}) copy-start(bf16[2,256,16,32]{1,0,3,2:T(2,128)(2,1)S(1)} %reshape_reshape.7) | copy-start | bytes 1572868
  89.8 6.4 copy-start.8
  110.0 74.5 %copy-start.40 = (f32[512]{0:T(512)}, f32[512]{0:T(512)S(1)}, u32[]{:S(2)}) copy-start(f32[512]{0:T(512)S(1)} %get-tuple-element.143) | copy-start | bytes 6148
  157.2 3.6 copy-start.11
  157.2 3.6 copy-start.49
  159.8 4.2 copy-start.20
  159.8 4.2 copy-start.26
  159.8 4.2 copy-start.29
  159.8 4.2 copy-start.47
  190.2 4.7 copy-start.16
  195.8 3.7 copy-start.35
  195.8 3.7 copy-start.37
  195.8 4.0 copy-start.42
  195.8 3.9 copy-start.43
  195.8 3.9 copy-start.44
  195.8 9.3 %copy-start.48 = (f32[512,16]{0,1:T(8,128)S(1)}, f32[512,16]{0,1:T(8,128)}, u32[]{:S(2)}) copy-start(f32[512,16]{0,1:T(8,128)} %get-tuple-element.144) | copy-start | bytes 98308
  195.8 9.3 %copy-start.74 = (f32[16]{0:T(128)S(1)}, f32[16]{0:T(128)}, u32[]{:S(2)}) copy-start(f32[16]{0:T(128)} %copy-done.73) | copy-start | bytes 196
  195.8 9.5 %copy-start.76 = (f32[16]{0:T(128)S(1)}, f32[16]{0:T(128)}, u32[]{:S(2)}) copy-start(f32[16]{0:T(128)} %param.24) | copy-start | bytes 196
  199.8 9.1 %copy-start.59 = (f32[512]{0:T(512)S(1)}, f32[512]{0:T(512)}, u32[]{:S(2)}) copy-start(f32[512]{0:T(512)} %mul.539) | copy-start | bytes 6148
  205.0 4.0 copy-start.5
  205.0 4.0 copy-start.6
  205.0 4.0 copy-start.7
  211.7 2.9 copy-start.71
  211.7 11.1 %copy-start.24 = (bf16[1024,16]{0,1:T(8,128)(2,1)S(1)}, bf16[1024,16]{0,1:T(8,128)(2,1)}, u32[]{:S(2)}) copy-start(bf16[1024,16]{0,1:T(8,128)(2,1)} %copy-done.23) | copy-start | bytes 98308
  226.8 92.7 %copy-start.13 = (f32[512,256]{1,0:T(8,128)S(1)}, f32[512,256]{1,0:T(8,128)}, u32[]{:S(2)}) copy-start(f32[512,256]{1,0:T(8,128)} %copy-done.12) | copy-start | bytes 1572868
  226.9 94.3 %copy-start.61 = (f32[256,1]{0,1:T(1,128)S(1)}, f32[256,1]{0,1:T(1,128)}, u32[]{:S(2)}) copy-start(f32[256,1]{0,1:T(1,128)} %copy-done.60) | copy-start | bytes 3076
  226.9 94.3 %copy-start.63 = (f32[256,1]{0,1:T(1,128)S(1)}, f32[256,1]{0,1:T(1,128)}, u32[]{:S(2)}) copy-start(f32[256,1]{0,1:T(1,128)} %copy-done.62) | copy-start | bytes 3076
  226.9 94.3 %copy-start.65 = (f32[256,1]{0,1:T(1,128)S(1)}, f32[256,1]{0,1:T(1,128)}, u32[]{:S(2)}) copy-start(f32[256,1]{0,1:T(1,128)} %copy-done.64) | copy-start | bytes 3076
  226.9 94.3 %copy-start.67 = (f32[256,1]{0,1:T(1,128)S(1)}, f32[256,1]{0,1:T(1,128)}, u32[]{:S(2)}) copy-start(f32[256,1]{0,1:T(1,128)} %copy-done.66) | copy-start | bytes 3076
  226.9 161.2 %reduce-scatter.10.cloned.1.call-start = ((), (), s32[]{:S(2)}) async-start(), calls=%async_computation.10 | async-start | bytes 1179648 | tf_op jit(solution)/shard_map/reduce_scatter | solution.py:196
  323.5 122.0 %reduce-scatter.12.cloned.1.call-start = ((), (), s32[]{:S(2)}) async-start(), calls=%async_computation.11 | async-start | bytes 73728 | tf_op jit(solution)/shard_map/reduce_scatter | solution.py:197
  324.6 193.3 %reduce-scatter.14.cloned.1.call-start = ((), (), s32[]{:S(2)}) async-start(), calls=%async_computation.12 | async-start | bytes 2359296 | tf_op jit(solution)/shard_map/reduce_scatter | solution.py:198
  328.1 261.9 %reduce-scatter.8.cloned.1.call-start = ((), (), s32[]{:S(2)}) async-start(), calls=%async_computation.9 | async-start | bytes 2359296 | tf_op jit(solution)/shard_map/reduce_scatter | solution.py:190
  331.4 2.3 copy-start.72
  331.4 330.7 %reduce-scatter.6.cloned.1.call-start = ((), (), s32[]{:S(2)}) async-start(), calls=%async_computation.8 | async-start | bytes 2359296 | tf_op jit(solution)/shard_map/reduce_scatter | solution.py:184
  333.8 41.4 %copy-start.68 = (f32[512]{0:T(512)S(1)}, f32[512]{0:T(512)}, u32[]{:S(2)}) copy-start(f32[512]{0:T(512)} %get-tuple-element.140) | copy-start | bytes 6148
  (22 other events, 28.1 us)
Sparse Core Ops, SparseCore 0:
  10.1 43.5 all-gather.3
  55.8 39.1 all-gather.5
  97.1 38.3 all-gather.7
  227.0 92.4 all-reduce.27
  323.6 64.4 reduce-scatter.9
  391.7 53.8 reduce-scatter.11
  449.6 68.2 reduce-scatter.13
  522.0 67.8 reduce-scatter.7
  594.1 67.9 reduce-scatter.5
where the time goes:
time: 679 us; the launch traced here: 669 us
  waiting for transfers between devices  401 us (59%)
  blocking collectives  122 us (18%)
  matrix products  76.5 us (11%)
  other arithmetic  32.2 us (5%)
  local copies, waits for them, and re-layouts  21.5 us (3%)
  between operations  15 us (2%)
    psum x1, waiting for transfers between devices, on_device(): summed = lax.psum(partial_out, ('head', 'tensor'))  92.6 us
    reduce_scatter x1, waiting for transfers between devices, on_device(): lax.psum_scatter(g_w_out.reshape(head_count, head_width, model_width), 'f...  72.4 us
    reduce_scatter x1, waiting for transfers between devices, on_device(): lax.psum_scatter(g_w_x.reshape(model_width, head_count, head_width), 'fsd...  72.1 us
    reduce_scatter x1, waiting for transfers between devices, on_device(): lax.psum_scatter(g_w_z.reshape(model_width, head_count, head_width), 'fsd...  72 us
    reduce_scatter x1, waiting for transfers between devices, on_device(): lax.psum_scatter(g_w_dt, 'fsdp', scatter_dimension=0, tiled=True)  55.8 us
    psum x1, blocking collectives, on_device(): lax.psum((g_norm_gain, g_conv_x.reshape(head_count, head_width, taps), g_...  38.1 us
    all_gather x1, blocking collectives, on_device(): lax.all_gather(weights[2], 'fsdp', axis=0, tiled=True)  32 us
    all_gather x1, blocking collectives, on_device(): lax.all_gather(weights[3], 'fsdp', axis=0, tiled=True)  28.3 us
  transfers between devices with their start and end apart: 9, of which 7 were waited for; matrix products, arithmetic and copies ran while one was open for 7% of the time, Pallas kernels for 0%

commit v1 on v0

--- a/solution.py
+++ b/solution.py
@@ -7,6 +7,12 @@
 SPAN = 256
 EPSILON = 1e-05
 PRECISE = lax.Precision.HIGHEST
+
+
+def add_all(x, mesh_axis):
+    shards = lax.all_gather(x, mesh_axis, axis=0, tiled=False)
+    total = shards.sum(axis=0)
+    return total
 
 
 def causal_conv(signal, kernel):
@@ -122,7 +128,7 @@
     scale_out = lax.rsqrt(square_sum / full_inner + EPSILON)[:, None]
     normed_out = (gated * scale_out * gain_flat).astype(jnp.bfloat16)
     partial_out = jnp.dot(normed_out, weight_out, preferred_element_type=jnp.float32)
-    summed = lax.psum(partial_out, ("head", "tensor"))
+    summed = add_all(partial_out, ("head", "tensor"))
     block_out = (summed + features).astype(jnp.bfloat16)
     again = (
         lax.all_gather(weights[0], "fsdp", axis=0, tiled=True),

time: 679 us -> 703 us (1.035)
  waiting for transfers between devices: 401 us -> 417 us
  other arithmetic: 32.2 us -> 41.9 us
    all_gather x0 -> x1, waiting for transfers between devices: none -> 57.6 us  [add_all(): shards = lax.all_gather(x, mesh_axis, axis=0, tiled=False)]
    psum x1, waiting for transfers between devices: 92.6 us -> 58.5 us  [on_device(): lax.psum(local_part, ('head', 'tensor'))]
    reduce_scatter x1, waiting for transfers between devices: 55.8 us -> 48.3 us  [on_device(): lax.psum_scatter(g_w_dt, 'fsdp', scatter_dimension=0, tiled=True)]
  transfers between devices with their start and end apart: 9 -> 10, of which waited for: 7 -> 8; matrix products, arithmetic and copies ran while one was open for 7% -> 8% of each run, Pallas kernels for 0% -> 0%
where the time goes in v1:
time: 703 us; the launch traced here: 693 us
  waiting for transfers between devices  417 us (59%)
  blocking collectives  122 us (17%)
  matrix products  75.1 us (11%)
  other arithmetic  41.9 us (6%)
  local copies, waits for them, and re-layouts  21 us (3%)
  between operations  15.4 us (2%)
    reduce_scatter x1, waiting for transfers between devices, on_device(): lax.psum_scatter(g_w_z.reshape(model_width, head_count, head_width), 'fsd...  72.1 us
    reduce_scatter x1, waiting for transfers between devices, on_device(): lax.psum_scatter(g_w_x.reshape(model_width, head_count, head_width), 'fsd...  72.1 us
    reduce_scatter x1, waiting for transfers between devices, on_device(): lax.psum_scatter(g_w_out.reshape(head_count, head_width, model_width), 'f...  72 us
    psum x1, waiting for transfers between devices, on_device(): lax.psum(local_part, ('head', 'tensor'))  58.5 us
    all_gather x1, waiting for transfers between devices, add_all(): shards = lax.all_gather(x, mesh_axis, axis=0, tiled=False)  57.6 us
    reduce_scatter x1, waiting for transfers between devices, on_device(): lax.psum_scatter(g_w_dt, 'fsdp', scatter_dimension=0, tiled=True)  48.3 us
    psum x1, blocking collectives, on_device(): lax.psum((g_norm_gain, g_conv_x.reshape(head_count, head_width, taps), g_...  38.3 us
    all_gather x1, blocking collectives, on_device(): lax.all_gather(weights[2], 'fsdp', axis=0, tiled=True)  31.7 us
  transfers between devices with their start and end apart: 10, of which 8 were waited for; matrix products, arithmetic and copies ran while one was open for 8% of the time, Pallas kernels for 0%

profile of v1, /device:TPU:0, one launch (start us, length us, event | category | flops | bytes accessed | tf_op | source)
XLA Modules:
  0.0 692.9 jit_solution(16199950182695180054)
XLA Ops:
  8.0 0.7 all-gather.8.cloned.1.call-update
  9.5 1.6 fusion.22
  11.6 28.1 %all_gather.28 = bf16[1024,16]{0,1:T(8,128)(2,1)S(1)} all-gather(bf16[128,16]{0,1:T(8,128)(2,1)} %param.20), channel_id=1, replica_groups=mesh['fsdp'=8,'head'=2,'tensor'=2] {'fsdp'}, dimensions={0}, use_global_device_ids=true | all-gather | bytes 36864 | tf_op jit(solution)/shard_map/all_gather | solution.py:100
  40.4 2.3 broadcast_multiply_fusion.8
  42.8 1.2 reduce-window.14
  44.4 0.7 fusion.91
  47.0 31.7 %all_gather.27 = bf16[1024,2,128]{2,1,0:T(2,128)(2,1)S(1)} all-gather(bf16[128,2,128]{2,1,0:T(2,128)(2,1)S(1)} %copy-done.22), channel_id=1, replica_groups=mesh['fsdp'=8,'head'=2,'tensor'=2] {'fsdp'}, dimensions={0}, use_global_device_ids=true | all-gather | bytes 589824 | tf_op jit(solution)/shard_map/all_gather | solution.py:99
  78.7 0.8 copy-done.7
  80.1 1.1 multiply_convert_fusion.3
  82.9 2.2 fusion.105
  85.1 0.9 copy-done.4
  86.0 1.6 multiply_convert_fusion.2
  88.0 1.3 convolution_add_fusion.3
  90.0 6.3 fusion.38
  96.4 0.8 copy.135
  97.3 1.3 copy.136
  98.6 3.6 multiply_reduce_fusion.9
  102.2 8.1 %psum.105 = f32[512]{0:T(512)S(1)} all-reduce(f32[512]{0:T(512)S(1)} %get-tuple-element.105), channel_id=1, replica_groups=mesh['fsdp'=8,'head'=2,'tensor'=2] {'head','tensor'}, use_global_device_ids=true, to_apply=%region_4.5 | all-reduce | flops 512 | bytes 4096 | tf_op jit(solution)/shard_map/psum | solution.py:127
  110.2 24.5 %all-gather.10.cloned.1.call-done = bf16[16,32,1024]{2,1,0:T(8,128)(2,1)} async-done(((bf16[16,32,128]{2,1,0:T(8,128)(2,1)}), bf16[16,32,1024]{2,1,0:T(8,128)(2,1)}) %all-gather.10.cloned.1.call-update) | async-done | bytes 1048592 | tf_op jit(solution)/shard_map/all_gather | solution.py:101
  134.7 3.9 multiply_reduce_fusion.3
  138.6 7.5 %psum.106 = f32[512]{0:T(512)S(1)} all-reduce(f32[512]{0:T(512)S(1)} %get-tuple-element.77), channel_id=1, replica_groups=mesh['fsdp'=8,'head'=2,'tensor'=2] {'head','tensor'}, use_global_device_ids=true, to_apply=%region_7.8 | all-reduce | flops 512 | bytes 4096 | tf_op jit(solution)/shard_map/psum | solution.py:150
  146.1 4.3 fusion.45
  150.4 1.3 copy.137
  151.8 2.9 reshape_reshape.8
  154.7 2.4 multiply_reduce_fusion.14
  157.0 3.2 convolution_bitcast_fusion.1
  160.5 1.9 convolution_bitcast_fusion.2
  163.0 11.3 %fusion.9 = (f32[2,256,16]{1,2,0:T(8,128)}, f32[2,256,16]{1,2,0:T(8,128)}, f32[2,256,16]{1,2,0:T(8,128)}, f32[2,256,256]{2,1,0:T(8,128)S(1)}) fusion(f32[2,256,16]{1,2,0:T(8,128)S(1)} %bitcast.243, f32[2,256,16]{1,2,0:T(8,128)S(1)} %copy-done.21, f32[2,256,256]{2,1,0:T(8,128)S(1)} %copy-done.16, pred[256,256]{1,0:T(8,128)(4,1)S(1)} %copy-done.24, ...), kind=kOutput, calls=%fused_computation.18 | convolution fusion | flops 836608000 | bytes 2850816 | tf_op jit(solution)/shard_map/transpose(jvp(clsh,cshp->clhp))/dot_general | solution.py:51
  174.3 0.9 multiply_reduce_fusion.2
  175.2 8.1 %fusion.41 = f32[2,256,16,32]{1,3,2,0:T(8,128)} fusion(f32[2,256,16]{1,2,0:T(8,128)S(1)} %bitcast.244, f32[2,256,16]{1,2,0:T(8,128)S(1)} %copy-done.21, f32[2,256,256]{2,1,0:T(8,128)S(1)} %copy-done.16, pred[256,256]{1,0:T(8,128)(4,1)S(1)} %copy-done.24, f32[2,256,16,32]{1,3,2,0:T(8,128)S(1)} %fusion.58, f32[2,16,32,256]{3,0,2,1:T(2,128)S(1)} %bitcast.208, ...), kind=kOutput, calls=%fused_computation.48 | convolution fusion | flops 816316416 | bytes 3833856 | tf_op jit(solution)/shard_map/transpose(jvp(clsh,cshp->clhp))/dot_general | solution.py:51
  183.3 1.4 convolution_add_fusion.2
  184.7 1.1 convolution_add_fusion.1
  186.8 0.9 add_bitcast_fusion.1
  187.7 5.0 reduce-window.16
  192.9 0.9 fusion.110
  194.5 0.8 reduce_sum.261
  195.4 2.0 copy.140
  197.5 1.1 copy.178
  198.5 2.5 copy.141
  201.1 4.2 multiply_reduce_fusion.7
  207.1 2.0 fusion.117
  209.2 2.1 fusion.118
  211.2 0.8 pad_maximum_fusion
  212.1 8.0 %all-reduce.25 = (bf16[512,16]{0,1:T(8,128)(2,1)S(1)}, f32[16]{0:T(128)S(1)}, f32[16]{0:T(128)S(1)}, f32[16]{0:T(128)S(1)}) all-reduce(f32[512,16]{0,1:T(8,128)S(1)} %get-tuple-element.104, f32[16]{0:T(128)S(1)} %get-tuple-element.103, f32[16]{0:T(128)S(1)} %negate_multiply_fusion, ...), channel_id=1, replica_groups=mesh['fsdp'=8,'head'=2,'tensor'=2] {'tensor'}, use_global_device_ids=true, to_apply=%region_15.16 | all-reduce | flops 8240 | bytes 49536 | tf_op jit(solution)/shard_map/psum | solution.py:160
  220.1 4.0 multiply_add_fusion
  224.2 58.5 %all-reduce.28.cloned.1.call-done = (f32[512,1024]{1,0:T(8,128)}, f32[512,256]{1,0:T(8,128)}) async-done(((f32[512,1024]{1,0:T(8,128)}, f32[512,256]{1,0:T(8,128)}), (f32[512,1024]{1,0:T(8,128)}, f32[512,256]{1,0:T(8,128)})) %all-reduce.28.cloned.1.call-update) | async-done | bytes 2621456 | tf_op jit(solution)/shard_map/psum | solution.py:179
  282.6 2.5 multiply_reduce_fusion.13
  285.5 1.6 fusion.95
  287.5 3.3 fusion.93
  290.9 1.0 fusion.82
  292.0 2.2 fusion.99
  294.2 3.4 fusion.92
  297.7 2.2 fusion.97
  300.1 2.6 fusion.31
  302.8 38.3 %all-reduce.23 = (f32[1024]{0:T(1024)}, f32[16,32,4]{1,0,2:T(8,128)S(1)}, f32[2,128,4]{1,2,0:T(4,128)}, f32[16]{0:T(128)}, f32[16]{0:T(128)}, /*index=5*/f32[16]{0:T(128)}, f32[16,32]{1,0:T(8,128)}) all-reduce(f32[1024]{0:T(1024)S(1)} %get-tuple-element.74, ...), channel_id=1, replica_groups=mesh['fsdp'=8,'head'=2,'tensor'=2] {'fsdp'}, use_global_device_ids=true, to_apply=%region_21.22 | all-reduce | flops 4656 | bytes 37248 | tf_op jit(solution)/shard_map/psum | solution.py:212
  341.6 10.1 %reduce-scatter.10.cloned.1.call-done = f32[128,256]{1,0:T(8,128)} async-done(((f32[1024,256]{1,0:T(8,128)}), f32[128,256]{1,0:T(8,128)}) %reduce-scatter.10.cloned.1.call-update) | async-done | bytes 131088 | tf_op jit(solution)/shard_map/reduce_scatter | solution.py:202
  351.7 1.6 reshape.276
  353.3 57.6 %all-gather.12.cloned.1.call-done = f32[2048,1024]{1,0:T(8,128)} async-done(((f32[512,1024]{1,0:T(8,128)}), f32[2048,1024]{1,0:T(8,128)}) %all-gather.12.cloned.1.call-update) | async-done | bytes 8388624 | tf_op jit(solution)/shard_map/all_gather | solution.py:13
  410.9 5.9 reduce_sum.225
  416.8 4.3 fusion.28
  421.1 48.3 %reduce-scatter.12.cloned.1.call-done = f32[128,16]{0,1:T(8,128)} async-done(((f32[1024,16]{0,1:T(8,128)}), f32[128,16]{0,1:T(8,128)}) %reduce-scatter.12.cloned.1.call-update) | async-done | bytes 8208 | tf_op jit(solution)/shard_map/reduce_scatter | solution.py:203
  469.4 72.1 %reduce-scatter.6.cloned.1.call-done = f32[128,16,32]{0,2,1:T(8,128)} async-done(((f32[1024,16,32]{0,2,1:T(8,128)}), f32[128,16,32]{0,2,1:T(8,128)}) %reduce-scatter.6.cloned.1.call-update) | async-done | bytes 262160 | tf_op jit(solution)/shard_map/reduce_scatter | solution.py:190
  541.5 72.0 %reduce-scatter.14.cloned.1.call-done = f32[16,32,128]{2,1,0:T(8,128)} async-done(((f32[16,32,1024]{2,1,0:T(8,128)}), f32[16,32,128]{2,1,0:T(8,128)}) %reduce-scatter.14.cloned.1.call-update) | async-done | bytes 262160 | tf_op jit(solution)/shard_map/reduce_scatter | solution.py:204
  613.5 72.1 %reduce-scatter.8.cloned.1.call-done = f32[128,16,32]{0,2,1:T(8,128)} async-done(((f32[1024,16,32]{0,2,1:T(8,128)}), f32[128,16,32]{0,2,1:T(8,128)}) %reduce-scatter.8.cloned.1.call-update) | async-done | bytes 262160 | tf_op jit(solution)/shard_map/reduce_scatter | solution.py:196
  (187 shorter events, 14.9 us)
Async XLA Ops:
  7.2 39.7 %copy-start.30 = (f32[16,32,4]{1,2,0:T(4,128)S(1)}, f32[16,32,4]{1,2,0:T(4,128)}, u32[]{:S(2)}) copy-start(f32[16,32,4]{1,2,0:T(4,128)} %param.21) | copy-start | bytes 24580
  7.2 39.8 %copy-start.22 = (bf16[128,2,128]{2,1,0:T(2,128)(2,1)S(1)}, bf16[128,2,128]{2,1,0:T(2,128)(2,1)}, u32[]{:S(2)}) copy-start(bf16[128,2,128]{2,1,0:T(2,128)(2,1)} %param.19) | copy-start | bytes 196612
  7.2 75.7 %all-gather.6.cloned.1.call-start = ((), (), s32[]{:S(2)}) async-start(), calls=%async_computation.5 | async-start | bytes 1179648 | tf_op jit(solution)/shard_map/all_gather | solution.py:97
  7.9 90.7 %all-gather.8.cloned.1.call-start = ((), (), s32[]{:S(2)}) async-start(), calls=%async_computation.6 | async-start | bytes 1179648 | tf_op jit(solution)/shard_map/all_gather | solution.py:98
  8.7 126.0 %all-gather.10.cloned.1.call-start = ((), (), s32[]{:S(2)}) async-start(), calls=%async_computation.7 | async-start | bytes 1179648 | tf_op jit(solution)/shard_map/all_gather | solution.py:101
  9.4 70.0 %copy-start = (bf16[512,1024]{1,0:T(8,128)(2,1)S(1)}, bf16[512,1024]{1,0:T(8,128)(2,1)}, u32[]{:S(2)}) copy-start(bf16[512,1024]{1,0:T(8,128)(2,1)} %param.14) | copy-start | bytes 3145732
  9.4 70.0 %copy-start.25 = (f32[1024]{0:T(1024)S(1)}, f32[1024]{0:T(1024)}, u32[]{:S(2)}) copy-start(f32[1024]{0:T(1024)} %param.16) | copy-start | bytes 12292
  9.4 273.2 %all-reduce.28.cloned.1.call-start = ((), (), s32[]{:S(2)}) async-start(), calls=%async_computation.14 | async-start | bytes 5242880 | tf_op jit(solution)/shard_map/psum | solution.py:179
  39.7 3.0 copy-start.18
  40.4 3.7 copy-start.56
  44.1 35.9 %copy-start.54 = (f32[2,128,4]{1,2,0:T(4,128)S(1)}, f32[2,128,4]{1,2,0:T(4,128)}, u32[]{:S(2)}) copy-start(f32[2,128,4]{1,2,0:T(4,128)} %param.22) | copy-start | bytes 12292
  44.2 45.8 %copy-start.20 = (f32[2,256,16]{1,2,0:T(8,128)}, f32[2,256,16]{1,2,0:T(8,128)S(1)}, u32[]{:S(2)}) copy-start(f32[2,256,16]{1,2,0:T(8,128)S(1)} %bitcast_bitcast_fusion.1) | copy-start | bytes 98308
  47.0 38.1 %copy-start.34 = (f32[512,1]{0,1:T(1,128)}, f32[512,1]{0,1:T(1,128)S(1)}, u32[]{:S(2)}) copy-start(f32[512,1]{0,1:T(1,128)S(1)} %get-tuple-element.131) | copy-start | bytes 6148
  47.0 38.1 %copy-start.36 = (f32[512,1]{0,1:T(1,128)}, f32[512,1]{0,1:T(1,128)S(1)}, u32[]{:S(2)}) copy-start(f32[512,1]{0,1:T(1,128)S(1)} %get-tuple-element.132) | copy-start | bytes 6148
  47.0 38.1 %copy-start.38 = (f32[512,1]{0,1:T(1,128)}, f32[512,1]{0,1:T(1,128)S(1)}, u32[]{:S(2)}) copy-start(f32[512,1]{0,1:T(1,128)S(1)} %get-tuple-element.133) | copy-start | bytes 6148
  47.0 38.1 %copy-start.40 = (f32[512,1]{0,1:T(1,128)}, f32[512,1]{0,1:T(1,128)S(1)}, u32[]{:S(2)}) copy-start(f32[512,1]{0,1:T(1,128)S(1)} %get-tuple-element.134) | copy-start | bytes 6148
  79.5 1.7 copy-start.57
  79.5 2.5 copy-start.53
  80.0 5.0 copy-start.44
  80.0 5.0 copy-start.46
  80.0 5.0 copy-start.48
  80.0 5.0 copy-start.50
  82.8 7.2 %copy-start.15 = (f32[2,256,256]{2,1,0:T(8,128)}, f32[2,256,256]{2,1,0:T(8,128)S(1)}, u32[]{:S(2)}) copy-start(f32[2,256,256]{2,1,0:T(8,128)S(1)} %fusion.116) | copy-start | bytes 1572868
  87.6 11.0 %copy-start.2 = (bf16[512,512]{1,0:T(8,128)(2,1)}, bf16[512,512]{1,0:T(8,128)(2,1)S(1)}, u32[]{:S(2)}) copy-start(bf16[512,512]{1,0:T(8,128)(2,1)S(1)} %get-tuple-element.107) | copy-start | bytes 1572868
  88.0 8.4 %copy-start.8 = (bf16[2,256,16,32]{1,0,3,2:T(2,128)(2,1)}, bf16[2,256,16,32]{1,0,3,2:T(2,128)(2,1)S(1)}, u32[]{:S(2)}) copy-start(bf16[2,256,16,32]{1,0,3,2:T(2,128)(2,1)S(1)} %reshape_reshape.7) | copy-start | bytes 1572868
  88.0 2.0 copy-start.23
  88.0 2.0 copy-start.31
  89.9 6.4 copy-start.5
  97.2 1.4 copy-start.42
  98.6 36.1 %copy-start.26 = (f32[512]{0:T(512)S(1)}, f32[512]{0:T(512)}, u32[]{:S(2)}) copy-start(f32[512]{0:T(512)} %mul.547) | copy-start | bytes 6148
  110.2 35.9 %copy-start.28 = (f32[512]{0:T(512)}, f32[512]{0:T(512)S(1)}, u32[]{:S(2)}) copy-start(f32[512]{0:T(512)S(1)} %get-tuple-element.142) | copy-start | bytes 6148
  154.6 5.6 copy-start.1
  154.6 5.6 copy-start.6
  157.0 3.5 copy-start.9
  157.0 3.5 copy-start.33
  160.5 2.5 copy-start.16
  160.5 2.5 copy-start.21
  160.5 2.5 copy-start.24
  160.5 2.5 copy-start.32
  197.4 3.6 copy-start.43
  201.1 4.3 copy-start.35
  201.1 4.3 copy-start.37
  201.1 4.3 copy-start.39
  201.1 4.3 copy-start.41
  205.9 1.2 copy-start.11
  207.1 2.0 copy-start.3
  207.1 2.0 copy-start.12
  209.2 2.1 copy-start.13
  209.2 2.1 copy-start.14
  209.2 10.9 %copy-start.19 = (bf16[1024,16]{0,1:T(8,128)(2,1)S(1)}, bf16[1024,16]{0,1:T(8,128)(2,1)}, u32[]{:S(2)}) copy-start(bf16[1024,16]{0,1:T(8,128)(2,1)} %copy-done.18) | copy-start | bytes 98308
  224.1 61.0 %copy-start.45 = (f32[256,1]{0,1:T(1,128)S(1)}, f32[256,1]{0,1:T(1,128)}, u32[]{:S(2)}) copy-start(f32[256,1]{0,1:T(1,128)} %copy-done.44) | copy-start | bytes 3076
  224.1 61.0 %copy-start.47 = (f32[256,1]{0,1:T(1,128)S(1)}, f32[256,1]{0,1:T(1,128)}, u32[]{:S(2)}) copy-start(f32[256,1]{0,1:T(1,128)} %copy-done.46) | copy-start | bytes 3076
  224.1 61.1 %copy-start.49 = (f32[256,1]{0,1:T(1,128)S(1)}, f32[256,1]{0,1:T(1,128)}, u32[]{:S(2)}) copy-start(f32[256,1]{0,1:T(1,128)} %copy-done.48) | copy-start | bytes 3076
  224.1 61.1 %copy-start.51 = (f32[256,1]{0,1:T(1,128)S(1)}, f32[256,1]{0,1:T(1,128)}, u32[]{:S(2)}) copy-start(f32[256,1]{0,1:T(1,128)} %copy-done.50) | copy-start | bytes 3076
  224.1 127.6 %reduce-scatter.10.cloned.1.call-start = ((), (), s32[]{:S(2)}) async-start(), calls=%async_computation.10 | async-start | bytes 1179648 | tf_op jit(solution)/shard_map/reduce_scatter | solution.py:202
  285.5 1.9 copy-start.27
  285.5 1.9 copy-start.29
  287.1 123.8 %all-gather.12.cloned.1.call-start = ((), (), s32[]{:S(2)}) async-start(), calls=%async_computation.13 | async-start | bytes 10485760 | tf_op jit(solution)/shard_map/all_gather | solution.py:13
  290.8 178.6 %reduce-scatter.12.cloned.1.call-start = ((), (), s32[]{:S(2)}) async-start(), calls=%async_computation.11 | async-start | bytes 73728 | tf_op jit(solution)/shard_map/reduce_scatter | solution.py:203
  291.9 249.6 %reduce-scatter.6.cloned.1.call-start = ((), (), s32[]{:S(2)}) async-start(), calls=%async_computation.8 | async-start | bytes 2359296 | tf_op jit(solution)/shard_map/reduce_scatter | solution.py:190
  294.1 319.3 %reduce-scatter.14.cloned.1.call-start = ((), (), s32[]{:S(2)}) async-start(), calls=%async_computation.12 | async-start | bytes 2359296 | tf_op jit(solution)/shard_map/reduce_scatter | solution.py:204
  297.6 2.4 copy-start.55
  297.6 388.0 %reduce-scatter.8.cloned.1.call-start = ((), (), s32[]{:S(2)}) async-start(), calls=%async_computation.9 | async-start | bytes 2359296 | tf_op jit(solution)/shard_map/reduce_scatter | solution.py:196
  410.9 5.9 copy-start.52
  (4 other events, 3.7 us)
Sparse Core Ops, SparseCore 0:
  10.0 43.5 all-gather.5
  55.7 38.4 all-gather.7
  96.3 38.3 all-gather.9
  224.2 58.3 all-reduce.27
  287.3 64.4 reduce-scatter.9
  353.7 57.1 all-gather.11
  414.6 54.7 reduce-scatter.11
  473.5 67.9 reduce-scatter.5
  545.6 67.8 reduce-scatter.13
  617.4 68.1 reduce-scatter.7
